TPU v7x, 32 devices: a whole 2x2x4 slice. The times are simulated.
32 devices in a mesh: grp: 2 (over y), tok: 4 (over z), feat: 4 (over x, core).
Axes of the slice: x: 2, y: 2, z: 4, core: 2. Of those that a mesh axis runs over, the one named last changes fastest.
Arguments:
- acts: bfloat16 [6144, 28672], P(('grp', 'tok'), 'feat'), parts along dimension 0, may hold values from -6 to 6
- grads: bfloat16 [6144, 8192], P(('grp', 'tok'), 'feat'), parts along dimension 0, may hold values from -6 to 6
- proj_in: bfloat16 [28672, 512], P('feat'), may hold values from -0.03125 to 0.03125
- proj_out: bfloat16 [8192, 512], P('feat'), may hold values from -0.0625 to 0.0625
- doc_lengths: int32 [8], P('grp'), parts along dimension 0, may hold values from 1 to 1536, 3072 in all
- doc_owner: int32 [8], P('grp'), parts along dimension 0, may hold values from 0 to 3, as said below
Outputs:
- doc_grads: float32 [8, 512, 512], P(('grp', 'tok'), 'feat'), parts along dimension 0
There are 2 independent parts, one for each index of `grp`. A program takes and returns all parts, laid end to end along the dimension named above; an argument that names none is the same for every part. Nothing has to cross between parts.
Inputs may be any that keep to these rules, and one draw needn't show every extreme that they name: `doc_lengths`: the lengths sum to 3072; the largest is exactly 1536. `doc_owner`: every index along tok owns exactly 1 documents.
All inputs are finite; a program needn't handle non-finite values.
Results may differ from a plain program's by a relative error of at most 0.0043.
Values may be sent and summed in bfloat16 or wider, within the bound.
A program may use at most 64 MiB of HBM per device.

v0:
```python
import jax
import jax.numpy as jnp
from jax import lax
from jax.sharding import PartitionSpec as P


def outer_sum(weight_cols, low_out, low_in):
    width = weight_cols.shape[1]
    row_share = low_out.shape[1]
    weighted = (low_out[:, None, :] * weight_cols[:, :, None]).reshape(
        low_out.shape[0], width * row_share
    )
    product = lax.dot_general(
        weighted, low_in, (((0,), (0,)), ((), ())), preferred_element_type=jnp.float32
    )
    return product.reshape(width, row_share, low_in.shape[1])


def shards(acts, grads, proj_in, proj_out, doc_lengths, doc_owner):
    tok_rows = acts.shape[0]
    doc_count = doc_lengths.shape[0]
    slot_count = doc_count // lax.axis_size("tok")
    part_in = jnp.dot(acts, proj_in, preferred_element_type=jnp.float32)
    part_out = jnp.dot(grads, proj_out, preferred_element_type=jnp.float32)
    full_in = lax.psum(part_in, "feat")
    grad_part = lax.psum_scatter(part_out, "feat", scatter_dimension=1, tiled=True)
    in_low = full_in.astype(jnp.bfloat16)
    out_low = grad_part.astype(jnp.bfloat16)
    doc_ends = jnp.cumsum(doc_lengths)
    doc_starts = doc_ends - doc_lengths
    doc_index = jnp.arange(doc_count, dtype=jnp.int32)
    same_owner = doc_owner[:, None] == doc_owner[None, :]
    earlier = doc_index[:, None] < doc_index[None, :]
    slot_rank = jnp.sum((same_owner & earlier).astype(jnp.int32), axis=0)
    target = doc_owner * slot_count + slot_rank
    matches = target[:, None] == doc_index[None, :]
    routing = matches.astype(jnp.bfloat16)
    own_first = lax.axis_index("tok") * slot_count
    position = lax.axis_index("tok") * tok_rows + jnp.arange(tok_rows, dtype=jnp.int32)
    member = (
        (position[:, None] >= doc_starts[None, :]) & (position[:, None] < doc_ends[None, :])
    ).astype(jnp.bfloat16)
    all_weights = jnp.dot(member, routing, preferred_element_type=jnp.float32).astype(jnp.bfloat16)
    totals = lax.psum_scatter(
        outer_sum(all_weights, out_low, in_low), "tok", scatter_dimension=0, tiled=True
    )
    slot_lengths = jnp.sum(jnp.where(matches, doc_lengths[:, None], 0), axis=0)
    own_lengths = lax.dynamic_slice_in_dim(slot_lengths, own_first, slot_count, 0)
    scaling = lax.rsqrt(own_lengths.astype(jnp.float32))
    return totals * scaling[:, None, None]


def solution(mesh):
    in_specs = (
        P(("grp", "tok"), "feat"),
        P(("grp", "tok"), "feat"),
        P("feat", None),
        P("feat", None),
        P("grp"),
        P("grp"),
    )
    out_specs = P(("grp", "tok"), "feat", None)
    return jax.shard_map(shards, mesh=mesh, in_specs=in_specs, out_specs=out_specs, check_vma=False)
```

profile of v0, /device:TPU:0, one launch (start us, length us, event | category | flops | bytes accessed | tf_op | source)
XLA Modules:
  0.0 109.7 jit_solution(2129140301364226923)
XLA Ops:
  6.5 0.0 copy-start
  6.5 0.0 copy-start.1
  6.5 0.0 reduce-scatter.3.cloned.1.call-start
  6.5 1.9 %copy-done = bf16[768,2048]{1,0:T(8,128)(2,1)S(1)} copy-done((bf16[768,2048]{1,0:T(8,128)(2,1)S(1)}, bf16[768,2048]{1,0:T(8,128)(2,1)}, u32[]{:S(2)}) %copy-start) | copy-done | bytes 3145752
  8.4 4.5 %fusion.15 = f32[768,512]{1,0:T(8,128)} fusion(bf16[768,2048]{1,0:T(8,128)(2,1)S(1)} %copy-done, bf16[2048,512]{1,0:T(8,128)(2,1)} %param.9), kind=kOutput, calls=%fused_computation.23 | convolution fusion | flops 1610612736 | bytes 6815744 | tf_op jit(solution)/shard_map/dot_general | solution.py:24
  13.0 0.0 reduce-scatter.3.cloned.1.call-update
  13.0 0.0 reduce-scatter.5.cloned.1.call-start
  13.0 0.0 copy-done.1
  13.1 0.1 convert_reduce_fusion
  13.1 0.0 copy-start.2
  13.1 11.6 %fusion.16 = f32[768,512]{1,0:T(8,128)} fusion(bf16[768,7168]{1,0:T(8,128)(2,1)} %param.6, bf16[7168,512]{1,0:T(8,128)(2,1)} %param.8), kind=kOutput, calls=%fused_computation.24 | convolution fusion | flops 5637144576 | bytes 19922944 | tf_op jit(solution)/shard_map/dot_general | solution.py:23
  24.8 0.0 copy-done.2
  24.8 0.2 reduce-window.8
  25.0 0.3 convolution_convert_fusion
  25.2 43.7 %all-reduce.1 = bf16[768,512]{1,0:T(8,128)(2,1)} all-reduce(f32[768,512]{1,0:T(8,128)} %fusion.16), channel_id=1, replica_groups=mesh['grp'=2,'tok'=4,'feat'=4] {'feat'}, use_global_device_ids=true, to_apply=%region_3.4 | all-reduce | flops 393216 | bytes 2359296 | tf_op jit(solution)/shard_map/psum | solution.py:25
  68.9 0.0 reduce-scatter.3.cloned.1.call-done
  68.9 1.0 convert_element_type.17
  70.0 0.1 copy.9
  70.1 2.7 %fusion = f32[4,128,512]{2,1,0:T(8,128)} fusion(bf16[768,512]{1,0:T(8,128)(2,1)} %all-reduce.1, bf16[768,4]{0,1:T(4,128)(2,1)S(1)} %convolution_convert_fusion, bf16[768,128]{0,1:T(8,128)(2,1)S(1)} %copy.9), kind=kOutput, calls=%fused_computation.1 | convolution fusion | flops 403046400 | bytes 2037760 | tf_op jit(solution)/shard_map/dot_general | solution.py:13
  72.8 0.0 reduce-scatter.5.cloned.1.call-update
  72.8 0.1 select_reduce_fusion
  72.9 0.6 dynamic_slice.3
  74.2 26.9 %reduce-scatter.5.cloned.1.call-done = f32[1,128,512]{2,1,0:T(8,128)} async-done(((f32[4,128,512]{2,1,0:T(8,128)}), f32[1,128,512]{2,1,0:T(8,128)}) %reduce-scatter.5.cloned.1.call-update) | async-done | bytes 262160 | tf_op jit(solution)/shard_map/reduce_scatter | solution.py:44
  101.1 1.7 %broadcast_multiply_fusion = f32[1,128,512]{2,1,0:T(8,128)} fusion(f32[1,128,512]{2,1,0:T(8,128)} %reduce-scatter.5.cloned.1.call-done, f32[]{:T(128)} %bitcast.6), kind=kLoop, calls=%fused_computation.8 | loop fusion | flops 65536 | bytes 524292 | tf_op jit(solution)/shard_map/mul | solution.py:50
  (3 shorter events, 0.0 us)
Async XLA Ops:
  6.5 1.9 %copy-start = (bf16[768,2048]{1,0:T(8,128)(2,1)S(1)}, bf16[768,2048]{1,0:T(8,128)(2,1)}, u32[]{:S(2)}) copy-start(bf16[768,2048]{1,0:T(8,128)(2,1)} %param.7) | copy-start | bytes 9437188
  6.5 6.5 %copy-start.1 = (s32[4]{0:T(128)S(1)}, s32[4]{0:T(128)}, u32[]{:S(2)}) copy-start(s32[4]{0:T(128)} %param.11) | copy-start | bytes 52
  6.5 62.4 %reduce-scatter.3.cloned.1.call-start = ((), (), s32[]{:S(2)}) async-start(), calls=%async_computation.2 | async-start | bytes 1966080 | tf_op jit(solution)/shard_map/reduce_scatter | solution.py:26
  13.0 88.2 %reduce-scatter.5.cloned.1.call-start = ((), (), s32[]{:S(2)}) async-start(), calls=%async_computation.3 | async-start | bytes 1310720 | tf_op jit(solution)/shard_map/reduce_scatter | solution.py:44
  13.1 11.6 %copy-start.2 = (s32[4]{0:T(128)S(1)}, s32[4]{0:T(128)}, u32[]{:S(2)}) copy-start(s32[4]{0:T(128)} %param.10) | copy-start | bytes 52
Sparse Core Ops, SparseCore 0:
  13.1 39.2 reduce-scatter.2
  73.0 28.1 reduce-scatter.4
where the time goes:
time: 110 us
  blocking collectives  43.7 us (40%)
  waiting for transfers between devices  27 us (25%)
  matrix products  19.1 us (17%)
  between operations  14.1 us (13%)
  other arithmetic  3.05 us (3%)
  local copies, waits for them, and re-layouts  2.62 us (2%)
    psum x1, blocking collectives, shards(): full_in = lax.psum(part_in, 'feat')  43.7 us
    reduce_scatter x1, waiting for transfers between devices, shards(): lax.psum_scatter(outer_sum(all_weights, out_low, in_low), 'tok', scatter_...  26.9 us
    dot_general x1, matrix products, shards(): part_in = jnp.dot(acts, proj_in, preferred_element_type=jnp.float32)  11.6 us
    dot_general x1, matrix products, shards(): part_out = jnp.dot(grads, proj_out, preferred_element_type=jnp.float32)  4.54 us
    dot_general x1, matrix products, outer_sum(): lax.dot_general(weighted, low_in, (((0,), (0,)), ((), ())), preferred_ele...  2.7 us
  transfers between devices with their start and end apart: 2, of which 1 were waited for; matrix products, arithmetic and copies ran while one was open for 12% of the time, Pallas kernels for 0%

commit v1 on v0

v1 whole, which is shorter than its diff:
```python
import functools
import jax
import jax.numpy as jnp
from jax import lax
from jax.experimental import pallas as pl
from jax.experimental.pallas import tpu as pltpu
from jax.sharding import PartitionSpec as P

MESH = pl.DeviceIdType.MESH
CORES = 2
HALVES = 2
OUT_STEPS = 2
IN_STEPS = 4


def kernel(
    toks, feats, len_ref, own_ref, acts_hbm, grads_hbm, pin_hbm, pout_hbm, res_ref,
    acts, grads, pin, pout,
    gp, gr, gown, gxs, gxr, gt, gm,
    ip, ir, isum, ixs, ixr, il, zf, zs, zr,
    a_sem, g_sem, pi_sem, po_sem,
    gs_send, gs_recv, gx_send, gx_recv, is_send, is_recv, ix_send, ix_recv,
    ig_send, ig_recv, z_send, z_recv,
):
    z = lax.axis_index("tok")
    f = lax.axis_index("feat")
    chips = feats // CORES
    x, c = f // CORES, lax.rem(f, CORES)
    oc = 1 - c
    sib = {"feat": x * CORES + oc}
    docs = len_ref.shape[0]
    slots = docs // toks
    rows, din = acts.shape
    dout = grads.shape[1]
    half = rows // HALVES
    width = gown.shape[2]
    rank = pin.shape[1]
    cols = rank // HALVES
    kin, kout = din // IN_STEPS, dout // OUT_STEPS

    def chip(dx):
        return lax.rem(x + dx, chips)

    def at_x(dx):
        return {"feat": chip(dx) * CORES + c}

    def tok(dz):
        return lax.rem(z + dz, toks)

    def g_copy(j):
        return (
            pltpu.make_async_copy(
                grads_hbm.at[:, pl.ds(j * kout, kout)], grads.at[:, pl.ds(j * kout, kout)], g_sem.at[j]
            ),
            pltpu.make_async_copy(
                pout_hbm.at[pl.ds(j * kout, kout)], pout.at[pl.ds(j * kout, kout)], po_sem.at[j]
            ),
        )

    def a_copy(r, j):
        return pltpu.make_async_copy(
            acts_hbm.at[pl.ds(r * half, half), pl.ds(j * kin, kin)],
            acts.at[pl.ds(r * half, half), pl.ds(j * kin, kin)],
            a_sem.at[r, j],
        )

    def p_copy(k, j):
        return pltpu.make_async_copy(
            pin_hbm.at[pl.ds(j * kin, kin), pl.ds(k * cols, cols)],
            pin.at[pl.ds(j * kin, kin), pl.ds(k * cols, cols)],
            pi_sem.at[k, j],
        )

    barrier = pltpu.get_barrier_semaphore()
    peers = [sib] + [at_x(dx) for dx in range(1, chips)] + [{"tok": tok(dz)} for dz in range(1, toks)]
    for peer in peers:
        pl.semaphore_signal(barrier, inc=1, device_id=peer, device_id_type=MESH)

    for j in range(OUT_STEPS):
        for copy in g_copy(j):
            copy.start()
    for j in range(IN_STEPS):
        p_copy(0, j).start()
        a_copy(0, j).start()
    for r in range(1, HALVES):
        for j in range(IN_STEPS):
            a_copy(r, j).start()
    for k in range(1, HALVES):
        for j in range(IN_STEPS):
            p_copy(k, j).start()

    def remote(src, dst, send, recv, device):
        return pltpu.make_async_remote_copy(
            src_ref=src, dst_ref=dst, send_sem=send, recv_sem=recv, device_id=device, device_id_type=MESH
        )

    def g_sib(h):
        return remote(gp.at[oc, h], gr.at[h], gs_send.at[h], gs_recv.at[h], sib)

    def g_x(h, dx):
        return remote(gxs.at[h, dx - 1], gxr.at[h, dx - 1], gx_send.at[h, dx - 1], gx_recv.at[h, dx - 1], at_x(dx))

    def i_sib(u):
        return remote(ip.at[u, oc], ir.at[u], is_send.at[u], is_recv.at[u], sib)

    def i_x(u, dx):
        return remote(ixs.at[u], ixr.at[u, dx - 1], ix_send.at[u, dx - 1], ix_recv.at[u, dx - 1], at_x(dx))

    def i_gather(u):
        place = il.at[u // HALVES, u % HALVES, c]
        return remote(place, place, ig_send.at[u], ig_recv.at[u], sib)

    def z_copy(k, dz):
        return remote(
            zs.at[k, tok(dz)], zr.at[k, dz - 1], z_send.at[k, dz - 1], z_recv.at[k, dz - 1], {"tok": tok(dz)}
        )

    def g_matmul(h):
        total = None
        for j in range(OUT_STEPS):
            if h == 0:
                for copy in g_copy(j):
                    copy.wait()
            term = jnp.dot(
                grads[h * half : (h + 1) * half, j * kout : (j + 1) * kout],
                pout[j * kout : (j + 1) * kout, :],
                preferred_element_type=jnp.float32,
            )
            total = term if total is None else total + term
        for b in range(feats):
            gp[b % CORES, h, b // CORES] = total[:, b * width : (b + 1) * width]

    def g_share(h):
        g_sib(h).wait_recv()
        gown[h] = gp[c, h, x] + gr[h, x]
        for dx in range(1, chips):
            gxs[h, dx - 1] = (gp[c, h, chip(dx)] + gr[h, chip(dx)]).astype(jnp.bfloat16)
            g_x(h, dx).start()

    def g_finish():
        for h in range(HALVES):
            full = gown[h]
            for dx in range(1, chips):
                g_x(h, dx).wait_recv()
                full = full + gxr[h, dx - 1].astype(jnp.float32)
            gt[:, h * half : (h + 1) * half] = full.T
        lengths = [len_ref[d] for d in range(docs)]
        owners = [own_ref[d] for d in range(docs)]
        starts, ends, targets = [], [], []
        running = jnp.int32(0)
        for d in range(docs):
            starts.append(running)
            running = running + lengths[d]
            ends.append(running)
            before = jnp.int32(0)
            for e in range(d):
                before = before + jnp.where(owners[e] == owners[d], 1, 0)
            targets.append(owners[d] * slots + before)
        position = z * rows + lax.broadcasted_iota(jnp.int32, (1, rows), 1)
        for o in range(docs):
            start, end = jnp.int32(0), jnp.int32(0)
            for d in range(docs):
                start = jnp.where(targets[d] == o, starts[d], start)
                end = jnp.where(targets[d] == o, ends[d], end)
            inside = (position >= start) & (position < end)
            gm[o * width : (o + 1) * width, :] = jnp.where(inside, gt[...], 0.0).astype(jnp.bfloat16)
        scales = []
        for s in range(slots):
            own_length = jnp.int32(0)
            for d in range(docs):
                own_length = jnp.where(targets[d] == z * slots + s, lengths[d], own_length)
            scales.append(lax.rsqrt(jnp.full((1, cols), own_length, jnp.int32).astype(jnp.float32)))
        return scales

    def i_matmul(u, steps):
        k, r = u // HALVES, u % HALVES
        for j in steps:
            if k == 0:
                a_copy(r, j).wait()
            if r == 0:
                p_copy(k, j).wait()
            term = jnp.dot(
                acts[r * half : (r + 1) * half, j * kin : (j + 1) * kin],
                pin[j * kin : (j + 1) * kin, k * cols : (k + 1) * cols],
                preferred_element_type=jnp.float32,
            )
            for core in range(CORES):
                piece = term[core * half // CORES : (core + 1) * half // CORES]
                if j == 0:
                    ip[u, core] = piece
                else:
                    ip[u, core] += piece

    def i_share(u):
        i_sib(u).wait_recv()
        total = ip[u, c] + ir[u]
        isum[u] = total
        ixs[u] = total.astype(jnp.bfloat16)
        for dx in range(1, chips):
            i_x(u, dx).start()

    def i_merge(u):
        full = isum[u]
        for dx in range(1, chips):
            i_x(u, dx).wait_recv()
            full = full + ixr[u, dx - 1].astype(jnp.float32)
        il[u // HALVES, u % HALVES, c] = full.astype(jnp.bfloat16)
        i_gather(u).start()

    def outer(k):
        for r in range(HALVES):
            i_gather(k * HALVES + r).wait_recv()
        part = jnp.dot(gm[...], il[k].reshape(rows, cols), preferred_element_type=jnp.float32)
        height = slots * width
        for o in range(toks):
            piece = part[o * height : (o + 1) * height]
            zf[k, o] = piece
            zs[k, o] = piece.astype(jnp.bfloat16)
        for dz in sorted(range(1, toks), key=lambda dz: -min(dz, toks - dz)):
            z_copy(k, dz).start()

    def finish(k, scales):
        total = zf[k, z]
        for dz in range(1, toks):
            z_copy(k, dz).wait_recv()
            total = total + zr[k, dz - 1].astype(jnp.float32)
        for s in range(slots):
            res_ref[s, :, k * cols : (k + 1) * cols] = total[s * width : (s + 1) * width] * scales[s]

    split = IN_STEPS // 2
    first, second = range(split), range(split, IN_STEPS)
    g_matmul(0)
    pl.semaphore_wait(barrier, len(peers))
    g_sib(0).start()
    g_matmul(1)
    g_sib(1).start()
    g_share(0)
    i_matmul(0, first)
    g_share(1)
    i_matmul(0, second)
    i_sib(0).start()
    i_matmul(1, first)
    i_share(0)
    i_matmul(1, second)
    i_sib(1).start()
    i_matmul(2, first)
    i_share(1)
    i_matmul(2, second)
    i_sib(2).start()
    i_matmul(3, first)
    i_share(2)
    i_matmul(3, second)
    i_sib(3).start()
    scales = g_finish()
    i_share(3)
    i_merge(0)
    i_merge(1)
    outer(0)
    i_merge(2)
    i_merge(3)
    outer(1)
    for k in range(HALVES):
        finish(k, scales)

    for h in range(HALVES):
        g_sib(h).wait_send()
        for dx in range(1, chips):
            g_x(h, dx).wait_send()
    for u in range(HALVES * HALVES):
        i_sib(u).wait_send()
        i_gather(u).wait_send()
        for dx in range(1, chips):
            i_x(u, dx).wait_send()
    for k in range(HALVES):
        for dz in range(1, toks):
            z_copy(k, dz).wait_send()


def shards(toks, feats, acts, grads, proj_in, proj_out, doc_lengths, doc_owner):
    rows, din = acts.shape
    dout = grads.shape[1]
    rank = proj_in.shape[1]
    docs = doc_lengths.shape[0]
    slots = docs // toks
    chips = feats // CORES
    width = rank // feats
    half, cols = rows // HALVES, rank // HALVES
    units = HALVES * HALVES
    share = half // CORES
    f32, bf16 = jnp.float32, jnp.bfloat16
    vmem, dma = pltpu.VMEM, pltpu.SemaphoreType.DMA
    away, far = chips - 1, toks - 1
    height = slots * width
    return pl.pallas_call(
        functools.partial(kernel, toks, feats),
        out_shape=jax.ShapeDtypeStruct((slots, width, rank), f32),
        in_specs=[pl.BlockSpec(memory_space=pltpu.SMEM)] * 2 + [pl.BlockSpec(memory_space=pl.ANY)] * 4,
        out_specs=pl.BlockSpec(memory_space=pltpu.VMEM),
        scratch_shapes=[
            vmem((rows, din), bf16),
            vmem((rows, dout), bf16),
            vmem((din, rank), bf16),
            vmem((dout, rank), bf16),
            vmem((CORES, HALVES, chips, half, width), f32),
            vmem((HALVES, chips, half, width), f32),
            vmem((HALVES, half, width), f32),
            vmem((HALVES, away, half, width), bf16),
            vmem((HALVES, away, half, width), bf16),
            vmem((width, rows), f32),
            vmem((docs * width, rows), bf16),
            vmem((units, CORES, share, cols), f32),
            vmem((units, share, cols), f32),
            vmem((units, share, cols), f32),
            vmem((units, share, cols), bf16),
            vmem((units, away, share, cols), bf16),
            vmem((HALVES, HALVES, CORES, share, cols), bf16),
            vmem((HALVES, toks, height, cols), f32),
            vmem((HALVES, toks, height, cols), bf16),
            vmem((HALVES, far, height, cols), bf16),
            dma((HALVES, IN_STEPS)),
            dma((OUT_STEPS,)),
            dma((HALVES, IN_STEPS)),
            dma((OUT_STEPS,)),
            dma((HALVES,)),
            dma((HALVES,)),
            dma((HALVES, away)),
            dma((HALVES, away)),
            dma((units,)),
            dma((units,)),
            dma((units, away)),
            dma((units, away)),
            dma((units,)),
            dma((units,)),
            dma((HALVES, far)),
            dma((HALVES, far)),
        ],
        compiler_params=pltpu.CompilerParams(
            collective_id=0, has_side_effects=True, vmem_limit_bytes=62 * 1024 * 1024
        ),
        name="projected_grads",
    )(doc_lengths, doc_owner, acts, grads, proj_in, proj_out)


def solution(mesh):
    in_specs = (
        P(("grp", "tok"), "feat"),
        P(("grp", "tok"), "feat"),
        P("feat", None),
        P("feat", None),
        P("grp"),
        P("grp"),
    )
    out_specs = P(("grp", "tok"), "feat", None)
    body = functools.partial(shards, mesh.shape["tok"], mesh.shape["feat"])
    return jax.shard_map(body, mesh=mesh, in_specs=in_specs, out_specs=out_specs, check_vma=False)
```

time: 110 us -> 44.3 us (0.40)
  blocking collectives: 43.7 us -> 0 us
  Pallas kernels: 0 us -> 42.5 us
  waiting for transfers between devices: 27 us -> 0 us
  matrix products: 19.1 us -> 0 us
  between operations: 14.1 us -> 0.01 us
  other arithmetic: 3.05 us -> 0 us
    psum x1 -> x0, blocking collectives: 43.7 us -> none  [shards(): full_in = lax.psum(part_in, 'feat')]
    pallas_call x0 -> x1, Pallas kernels: none -> 42.5 us  [shards(): pl.pallas_call(functools.partial(kernel, toks, feats), out_shape=jax.Shap...]
    reduce_scatter x2 -> x0, waiting for transfers between devices: 26.9 us -> none  [the longest x1 26.9 us: shards(): lax.psum_scatter(outer_sum(all_weights, out_low, in_low), 'tok', scatter_...]
    dot_general x4 -> x0, matrix products: 19.1 us -> none  [the longest x1 11.6 us: shards(): part_in = jnp.dot(acts, proj_in, preferred_element_type=jnp.float32)]
    mul x1 -> x0, other arithmetic: 1.67 us -> none  [shards(): return totals * scaling[:, None, None]]
  transfers between devices with their start and end apart: 2 -> 0, of which waited for: 1 -> 0; matrix products, arithmetic and copies ran while one was open for 12% -> 0% of each run, Pallas kernels for 0% -> 0%
where the time goes in v1:
time: 44.3 us; the launch traced here: 44.1 us
  Pallas kernels  42.5 us (96%)
  local copies, waits for them, and re-layouts  1.67 us (4%)
    pallas_call x1, Pallas kernels, shards(): pl.pallas_call(functools.partial(kernel, toks, feats), out_shape=jax.Shap...  42.5 us
    unnamed x1, local copies, waits for them, and re-layouts  1.67 us

profile of v1, /device:TPU:0, one launch (start us, length us, event | category | flops | bytes accessed | tf_op | source)
XLA Modules:
  0.0 44.1 jit_solution(18006024703707326510)
XLA Ops:
  0.0 42.5 %projected_grads.1 = f32[1,128,512]{2,1,0:T(8,128)} custom-call(s32[4]{0:T(128)} %len_ref.1, s32[4]{0:T(128)} %own_ref.1, bf16[768,7168]{1,0:T(8,128)(2,1)} %acts_hbm.1, bf16[768,2048]{1,0:T(8,128)(2,1)} %grads_hbm.1, bf16[7168,512]{1,0:T(8,128)(2,1)} %pin_hbm.1, bf16[2048,512]{1,0:T(8,128)(2,1)} %pout_hbm.1), custom_call_target="tpu_custom_call" | custom-call | tf_op jit(solution)/shard_map/projected_grads/pallas_call | solution.py:294
  42.5 1.7 %copy.8 = f32[1,128,512]{2,1,0:T(8,128)} copy(f32[1,128,512]{2,1,0:T(8,128)} %projected_grads.1) | data formatting | bytes 524288

commit v2 on v1

--- a/solution.py
+++ b/solution.py
@@ -9,8 +9,10 @@
 MESH = pl.DeviceIdType.MESH
 CORES = 2
 HALVES = 2
+CHUNKS = 4
 OUT_STEPS = 2
-IN_STEPS = 4
+IN_STEPS = 7
+AHEAD = 8
 
 
 def kernel(
@@ -35,7 +37,8 @@
     half = rows // HALVES
     width = gown.shape[2]
     rank = pin.shape[1]
-    cols = rank // HALVES
+    cols = rank // CHUNKS
+    units = CHUNKS * HALVES
     kin, kout = din // IN_STEPS, dout // OUT_STEPS
 
     def chip(dx):
@@ -47,14 +50,16 @@
     def tok(dz):
         return lax.rem(z + dz, toks)
 
-    def g_copy(j):
-        return (
-            pltpu.make_async_copy(
-                grads_hbm.at[:, pl.ds(j * kout, kout)], grads.at[:, pl.ds(j * kout, kout)], g_sem.at[j]
-            ),
-            pltpu.make_async_copy(
-                pout_hbm.at[pl.ds(j * kout, kout)], pout.at[pl.ds(j * kout, kout)], po_sem.at[j]
-            ),
+    def g_copy(h, j):
+        return pltpu.make_async_copy(
+            grads_hbm.at[pl.ds(h * half, half), pl.ds(j * kout, kout)],
+            grads.at[pl.ds(h * half, half), pl.ds(j * kout, kout)],
+            g_sem.at[h, j],
+        )
+
+    def q_copy(j):
+        return pltpu.make_async_copy(
+            pout_hbm.at[pl.ds(j * kout, kout)], pout.at[pl.ds(j * kout, kout)], po_sem.at[j]
         )
 
     def a_copy(r, j):
@@ -64,11 +69,9 @@
             a_sem.at[r, j],
         )
 
-    def p_copy(k, j):
+    def p_copy(j):
         return pltpu.make_async_copy(
-            pin_hbm.at[pl.ds(j * kin, kin), pl.ds(k * cols, cols)],
-            pin.at[pl.ds(j * kin, kin), pl.ds(k * cols, cols)],
-            pi_sem.at[k, j],
+            pin_hbm.at[pl.ds(j * kin, kin)], pin.at[pl.ds(j * kin, kin)], pi_sem.at[j]
         )
 
     barrier = pltpu.get_barrier_semaphore()
@@ -76,18 +79,22 @@
     for peer in peers:
         pl.semaphore_signal(barrier, inc=1, device_id=peer, device_id_type=MESH)
 
-    for j in range(OUT_STEPS):
-        for copy in g_copy(j):
+    loads = [copy for j in range(OUT_STEPS) for copy in (q_copy(j), g_copy(0, j))]
+    loads += [g_copy(h, j) for h in range(1, HALVES) for j in range(OUT_STEPS)]
+    loads += [copy for j in range(IN_STEPS) for copy in (p_copy(j), a_copy(0, j))]
+    loads += [a_copy(r, j) for r in range(1, HALVES) for j in range(IN_STEPS)]
+    issued = [0]
+
+    def issue(count):
+        for copy in loads[issued[0] : issued[0] + count]:
             copy.start()
-    for j in range(IN_STEPS):
-        p_copy(0, j).start()
-        a_copy(0, j).start()
-    for r in range(1, HALVES):
-        for j in range(IN_STEPS):
-            a_copy(r, j).start()
-    for k in range(1, HALVES):
-        for j in range(IN_STEPS):
-            p_copy(k, j).start()
+        issued[0] += count
+
+    def arrive(copy):
+        copy.wait()
+        issue(1)
+
+    issue(AHEAD)
 
     def remote(src, dst, send, recv, device):
         return pltpu.make_async_remote_copy(
@@ -119,8 +126,8 @@
         total = None
         for j in range(OUT_STEPS):
             if h == 0:
-                for copy in g_copy(j):
-                    copy.wait()
+                arrive(q_copy(j))
+            arrive(g_copy(h, j))
             term = jnp.dot(
                 grads[h * half : (h + 1) * half, j * kout : (j + 1) * kout],
                 pout[j * kout : (j + 1) * kout, :],
@@ -172,24 +179,30 @@
             scales.append(lax.rsqrt(jnp.full((1, cols), own_length, jnp.int32).astype(jnp.float32)))
         return scales
 
-    def i_matmul(u, steps):
-        k, r = u // HALVES, u % HALVES
+    def i_matmul(p, r, steps):
+        wide = rank // HALVES
+        per = CHUNKS // HALVES
         for j in steps:
-            if k == 0:
-                a_copy(r, j).wait()
-            if r == 0:
-                p_copy(k, j).wait()
+            if p == 0:
+                if r == 0:
+                    arrive(p_copy(j))
+                arrive(a_copy(r, j))
             term = jnp.dot(
                 acts[r * half : (r + 1) * half, j * kin : (j + 1) * kin],
-                pin[j * kin : (j + 1) * kin, k * cols : (k + 1) * cols],
+                pin[j * kin : (j + 1) * kin, p * wide : (p + 1) * wide],
                 preferred_element_type=jnp.float32,
             )
-            for core in range(CORES):
-                piece = term[core * half // CORES : (core + 1) * half // CORES]
-                if j == 0:
-                    ip[u, core] = piece
-                else:
-                    ip[u, core] += piece
+            for q in range(per):
+                u = (p * per + q) * HALVES + r
+                for core in range(CORES):
+                    piece = term[core * half // CORES : (core + 1) * half // CORES, q * cols : (q + 1) * cols]
+                    if j == 0:
+                        ip[u, core] = piece
+                    else:
+                        ip[u, core] += piece
+        if steps[-1] == IN_STEPS - 1:
+            for q in range(per):
+                i_sib((p * per + q) * HALVES + r).start()
 
     def i_share(u):
         i_sib(u).wait_recv()
@@ -235,43 +248,49 @@
     g_matmul(1)
     g_sib(1).start()
     g_share(0)
-    i_matmul(0, first)
+    i_matmul(0, 0, first)
     g_share(1)
-    i_matmul(0, second)
-    i_sib(0).start()
-    i_matmul(1, first)
+    i_matmul(0, 0, second)
+    i_matmul(0, 1, first)
     i_share(0)
-    i_matmul(1, second)
-    i_sib(1).start()
-    i_matmul(2, first)
+    i_matmul(0, 1, second)
+    i_matmul(1, 0, first)
     i_share(1)
-    i_matmul(2, second)
-    i_sib(2).start()
-    i_matmul(3, first)
     i_share(2)
-    i_matmul(3, second)
-    i_sib(3).start()
+    i_share(3)
+    i_matmul(1, 0, second)
+    i_matmul(1, 1, first)
+    i_share(4)
+    i_matmul(1, 1, second)
     scales = g_finish()
-    i_share(3)
     i_merge(0)
     i_merge(1)
+    i_share(5)
+    i_share(6)
+    i_share(7)
     outer(0)
     i_merge(2)
     i_merge(3)
     outer(1)
-    for k in range(HALVES):
+    i_merge(4)
+    i_merge(5)
+    outer(2)
+    i_merge(6)
+    i_merge(7)
+    outer(3)
+    for k in range(CHUNKS):
         finish(k, scales)
 
     for h in range(HALVES):
         g_sib(h).wait_send()
         for dx in range(1, chips):
             g_x(h, dx).wait_send()
-    for u in range(HALVES * HALVES):
+    for u in range(units):
         i_sib(u).wait_send()
         i_gather(u).wait_send()
         for dx in range(1, chips):
             i_x(u, dx).wait_send()
-    for k in range(HALVES):
+    for k in range(CHUNKS):
         for dz in range(1, toks):
             z_copy(k, dz).wait_send()
 
@@ -284,8 +303,8 @@
     slots = docs // toks
     chips = feats // CORES
     width = rank // feats
-    half, cols = rows // HALVES, rank // HALVES
-    units = HALVES * HALVES
+    half, cols = rows // HALVES, rank // CHUNKS
+    units = CHUNKS * HALVES
     share = half // CORES
     f32, bf16 = jnp.float32, jnp.bfloat16
     vmem, dma = pltpu.VMEM, pltpu.SemaphoreType.DMA
@@ -313,13 +332,13 @@
             vmem((units, share, cols), f32),
             vmem((units, share, cols), bf16),
             vmem((units, away, share, cols), bf16),
-            vmem((HALVES, HALVES, CORES, share, cols), bf16),
-            vmem((HALVES, toks, height, cols), f32),
-            vmem((HALVES, toks, height, cols), bf16),
-            vmem((HALVES, far, height, cols), bf16),
+            vmem((CHUNKS, HALVES, CORES, share, cols), bf16),
+            vmem((CHUNKS, toks, height, cols), f32),
+            vmem((CHUNKS, toks, height, cols), bf16),
+            vmem((CHUNKS, far, height, cols), bf16),
             dma((HALVES, IN_STEPS)),
-            dma((OUT_STEPS,)),
-            dma((HALVES, IN_STEPS)),
+            dma((HALVES, OUT_STEPS)),
+            dma((IN_STEPS,)),
             dma((OUT_STEPS,)),
             dma((HALVES,)),
             dma((HALVES,)),
@@ -331,8 +350,8 @@
             dma((units, away)),
             dma((units,)),
             dma((units,)),
-            dma((HALVES, far)),
-            dma((HALVES, far)),
+            dma((CHUNKS, far)),
+            dma((CHUNKS, far)),
         ],
         compiler_params=pltpu.CompilerParams(
             collective_id=0, has_side_effects=True, vmem_limit_bytes=62 * 1024 * 1024

time: 44.3 us -> 39.6 us (0.89)
  Pallas kernels: 42.5 us -> 37.8 us
    pallas_call x1, Pallas kernels: 42.5 us -> 37.8 us  [shards(): pl.pallas_call(functools.partial(kernel, toks, feats), out_shape=jax.Shap...]
where the time goes in v2:
time: 39.6 us; the launch traced here: 39.5 us
  Pallas kernels  37.8 us (95%)
  local copies, waits for them, and re-layouts  1.67 us (4%)
    pallas_call x1, Pallas kernels, shards(): pl.pallas_call(functools.partial(kernel, toks, feats), out_shape=jax.Shap...  37.8 us
    unnamed x1, local copies, waits for them, and re-layouts  1.67 us

profile of v2, /device:TPU:0, one launch (start us, length us, event | category | flops | bytes accessed | tf_op | source)
XLA Modules:
  0.0 39.5 jit_solution(8090527260822191634)
XLA Ops:
  0.0 37.8 %projected_grads.1 = f32[1,128,512]{2,1,0:T(8,128)} custom-call(s32[4]{0:T(128)} %len_ref.1, s32[4]{0:T(128)} %own_ref.1, bf16[768,7168]{1,0:T(8,128)(2,1)} %acts_hbm.1, bf16[768,2048]{1,0:T(8,128)(2,1)} %grads_hbm.1, bf16[7168,512]{1,0:T(8,128)(2,1)} %pin_hbm.1, bf16[2048,512]{1,0:T(8,128)(2,1)} %pout_hbm.1), custom_call_target="tpu_custom_call" | custom-call | tf_op jit(solution)/shard_map/projected_grads/pallas_call | solution.py:313
  37.8 1.7 %copy.8 = f32[1,128,512]{2,1,0:T(8,128)} copy(f32[1,128,512]{2,1,0:T(8,128)} %projected_grads.1) | data formatting | bytes 524288
